TPU v7x, 512 devices: a whole 4x8x8 slice. The times are simulated.
512 devices in a mesh: dp: 64 (over y, z), mix: 8 (over x, core).
Axes of the slice: x: 4, y: 8, z: 8, core: 2. Of those that a mesh axis runs over, the one named last changes fastest.
Arguments:
- matrix: float32 [131072, 1024], P(('dp', 'mix'))
- counts: int32 [64, 8], P('dp'), may hold values from 0 to 256, as said below
- sign_bits: int32 [131072], P(('dp', 'mix')), may hold values from 0 to 1
- samples: int32 [64, 32], P('dp'), may hold values from 0 to 1023
- gaussian: float32 [1024, 64], replicated, may hold values from -6 to 6
Outputs:
- leverage: float32 [131072], P(('dp', 'mix'))
Inputs may be any that keep to these rules, and one draw needn't show every extreme that they name: In each dp index g, the counts of mix indices 0 to m - 1 sum to m * 128 plus a number of magnitude at most 64, which reaches that magnitude for some m in every g; all 8 counts sum to 1024.
All inputs are finite; a program needn't handle non-finite values.
Results may differ from a plain program's by a relative error of at most 0.0003.
Values sent between devices are 32-bit elements; how exact they have to be, the bound alone decides.
A program may use at most 64 MiB of HBM per device.

v0:
```python
import math

import jax
import jax.numpy as jnp
from jax import lax
from jax.sharding import PartitionSpec as P


def passed_along(block, axis, distance):
    devices = range(lax.axis_size(axis))
    route = [(i - distance, i) for i in devices if i - distance in devices]
    return lax.ppermute(block, axis, route)


def partner_2(value, axis, bit):
    mask = 2**bit
    pairs = [(source, source ^ mask) for source in range(lax.axis_size(axis))]
    return lax.ppermute(value, axis, pairs)


def hadamard(row_ids, col_ids):
    correlation = jnp.bitwise_and(row_ids[:, None], col_ids[None, :])
    parity = jnp.zeros(correlation.shape, jnp.int32)
    for bit_number in range(16):
        parity = jnp.bitwise_xor(
            parity, jnp.bitwise_and(jnp.right_shift(correlation, bit_number), 1)
        )
    return (1 - 2 * parity).astype(jnp.float32)


def shards(matrix, counts, sign_bits, samples, gaussian):
    capacity = matrix.shape[0]
    col_count = matrix.shape[1]
    slot_count = capacity // 2
    half_slots = slot_count // 2
    mix_count = lax.axis_size("mix")
    dp_count = lax.axis_size("dp")
    mix_index = lax.axis_index("mix")
    group_counts = counts[0]
    member = jnp.arange(mix_count, dtype=jnp.int32)
    first_row = jnp.sum(jnp.where(member < mix_index, group_counts, 0))
    own_count = jnp.sum(jnp.where(member == mix_index, group_counts, 0))
    lead_gap = first_row - mix_index * slot_count
    trail_gap = first_row + own_count - (mix_index + 1) * slot_count
    slot_ids = jnp.arange(capacity, dtype=jnp.int32)
    masked = jnp.where((slot_ids < own_count)[:, None], matrix, 0.0)
    signed = masked * (2 * sign_bits - 1).astype(jnp.float32)[:, None]
    picked = samples[0]
    pick_count = picked.shape[0]
    sketch_scale = 1.0 / math.sqrt(mix_count * slot_count * pick_count)
    offsets = jnp.arange(half_slots, dtype=jnp.int32)
    upward = lax.dynamic_slice_in_dim(signed, slot_count - lead_gap, half_slots, 0)
    upward = jnp.where((offsets < trail_gap)[:, None], upward, 0.0)
    downward = jnp.where((offsets < -lead_gap)[:, None], signed[:half_slots], 0.0)
    from_prev = passed_along(upward, "mix", 1)
    from_next = passed_along(downward, "mix", -1)
    positions = jnp.arange(slot_count, dtype=jnp.int32)
    padded_own = jnp.concatenate([jnp.zeros((half_slots, col_count), jnp.float32), signed], axis=0)
    own_rows = lax.dynamic_slice_in_dim(padded_own, half_slots - lead_gap, slot_count, 0)
    keep_mask = (positions - lead_gap >= 0) & (positions - lead_gap < own_count)
    own_rows = jnp.where(keep_mask[:, None], own_rows, 0.0)
    lower_part = jnp.concatenate(
        [from_prev, jnp.zeros((half_slots, col_count), jnp.float32)], axis=0
    )
    lower_part = jnp.where((positions < lead_gap)[:, None], lower_part, 0.0)
    padded_next = jnp.concatenate(
        [jnp.zeros((slot_count + half_slots, col_count), jnp.float32), from_next], axis=0
    )
    upper_part = lax.dynamic_slice_in_dim(padded_next, half_slots - trail_gap, slot_count, 0)
    upper_part = jnp.where((positions - slot_count - trail_gap >= 0)[:, None], upper_part, 0.0)
    relaid = own_rows + lower_part + upper_part
    local_table = hadamard(positions, positions)
    mixed_rows = jnp.dot(local_table, relaid, precision=lax.Precision.HIGHEST)
    for bit_number in range(mix_count.bit_length() - 1):
        partner = partner_2(mixed_rows, "mix", bit_number)
        upper_half = jnp.bitwise_and(jnp.right_shift(mix_index, bit_number), 1) == 1
        mixed_rows = jnp.where(upper_half, partner - mixed_rows, mixed_rows + partner)
    selector = (picked[:, None] == mix_index * slot_count + positions[None, :]).astype(jnp.float32)
    partial_sketch = jnp.dot(selector, mixed_rows, precision=lax.Precision.HIGHEST) * sketch_scale
    sketch = lax.psum(partial_sketch, "mix")
    gram_share = lax.psum_scatter(
        jnp.dot(sketch.T, sketch, precision=lax.Precision.HIGHEST),
        "dp",
        scatter_dimension=0,
        tiled=True,
    )
    gram_matrix = lax.all_gather(gram_share, "dp", axis=0, tiled=True)
    factor_lower = jnp.linalg.cholesky(gram_matrix)
    solved = jax.scipy.linalg.solve_triangular(factor_lower, gaussian, trans=1, lower=True)
    norm_factor = dp_count * mix_count * slot_count / (col_count * gaussian.shape[1])
    projected = jnp.dot(masked, solved, precision=lax.Precision.HIGHEST)
    return jnp.sum(projected * projected, axis=1) * norm_factor


def solution(mesh):
    in_specs = (P(("dp", "mix"), None), P("dp", None), P(("dp", "mix")), P("dp", None), P())
    out_specs = P(("dp", "mix"))
    return jax.shard_map(shards, mesh=mesh, in_specs=in_specs, out_specs=out_specs, check_vma=False)
```

profile of v0, /device:TPU:1, one launch (start us, length us, event | category | flops | bytes accessed | tf_op | source)
XLA Modules:
  0.0 819.2 jit_solution(2415782914848890410)
XLA Ops:
  12.8 4.5 collective-permute-start
  17.3 5.6 collective-permute-start.1
  29.8 3.1 collective-permute-start.3
  32.9 12.1 %collective-permute-done.3 = f32[128,1024]{1,0:T(8,128)S(1)} collective-permute-done((f32[128,1024]{1,0:T(8,128)S(1)}, f32[128,1024]{1,0:T(8,128)S(1)}, u32[]{:S(2)}, u32[]{:S(2)}) %collective-permute-start.3) | collective-permute-done | bytes 524320 | tf_op jit(solution)/shard_map/ppermute | solution.py:18
  45.1 4.4 collective-permute-start.4
  49.5 11.5 %collective-permute-done.4 = f32[128,1024]{1,0:T(8,128)S(1)} collective-permute-done((f32[128,1024]{1,0:T(8,128)S(1)}, f32[128,1024]{1,0:T(8,128)S(1)}, u32[]{:S(2)}, u32[]{:S(2)}) %collective-permute-start.4) | collective-permute-done | bytes 524320 | tf_op jit(solution)/shard_map/ppermute | solution.py:18
  62.1 74.9 %all-reduce.6.cloned.1.call-done = f32[32,1024]{1,0:T(8,128)} async-done(((f32[32,1024]{1,0:T(8,128)}), f32[32,1024]{1,0:T(8,128)}) %all-reduce.6.cloned.1.call-update) | async-done | bytes 131088 | tf_op jit(solution)/shard_map/psum | solution.py:80
  137.0 6.4 fusion.175
  143.4 246.2 %reduce-scatter.4.cloned.1.call-done = f32[16,1024]{1,0:T(8,128)} async-done(((f32[1024,1024]{1,0:T(8,128)}), f32[16,1024]{1,0:T(8,128)}) %reduce-scatter.4.cloned.1.call-update) | async-done | bytes 65552 | tf_op jit(solution)/shard_map/reduce_scatter | solution.py:81
  389.7 87.6 %all-gather.2.cloned.1.call-done = f32[1024,1024]{1,0:T(8,128)} async-done(((f32[16,1024]{1,0:T(8,128)}), f32[1024,1024]{1,0:T(8,128)}) %all-gather.2.cloned.1.call-update) | async-done | bytes 4194320 | tf_op jit(solution)/shard_map/all_gather | solution.py:87
  477.3 5.6 copy.10
  482.9 4.4 fusion
  489.3 11.7 %cholesky.225 = f32[128,128]{1,0:T(8,128)S(1)} custom-call(f32[128,128]{1,0:T(8,128)S(1)} %cholesky.583), custom_call_target="Cholesky" | custom-call | tf_op jit(solution)/shard_map/jit(cholesky)/cholesky | solution.py:88
  501.0 2.5 cholesky.257
  503.5 9.8 %custom-call.63 = f32[1,128,128]{1,2,0:T(8,128)S(1)} custom-call(f32[1,128,128]{2,1,0:T(8,128)S(1)} %get-tuple-element.48), custom_call_target="InvertDiagBlocksLowerTriangular" | custom-call | tf_op jit(solution)/shard_map/jit(cholesky)/cholesky | solution.py:88
  513.3 2.4 constant_dynamic-update-slice_fusion.29
  517.3 12.2 %cholesky.246 = f32[128,128]{1,0:T(8,128)S(1)} custom-call(f32[128,128]{1,0:T(8,128)S(1)} %cholesky.587), custom_call_target="Cholesky" | custom-call | tf_op jit(solution)/shard_map/jit(cholesky)/cholesky | solution.py:88
  531.4 9.8 %custom-call.64 = f32[1,128,128]{1,2,0:T(8,128)S(1)} custom-call(f32[1,128,128]{2,1,0:T(8,128)S(1)} %get-tuple-element.45), custom_call_target="InvertDiagBlocksLowerTriangular" | custom-call | tf_op jit(solution)/shard_map/jit(cholesky)/cholesky | solution.py:88
  544.6 11.7 %cholesky.471 = f32[128,128]{1,0:T(8,128)S(1)} custom-call(f32[128,128]{1,0:T(8,128)S(1)} %cholesky.592), custom_call_target="Cholesky" | custom-call | tf_op jit(solution)/shard_map/jit(cholesky)/cholesky | solution.py:88
  557.6 9.8 %custom-call.65 = f32[1,128,128]{1,2,0:T(8,128)S(1)} custom-call(f32[1,128,128]{2,1,0:T(8,128)S(1)} %get-tuple-element.42), custom_call_target="InvertDiagBlocksLowerTriangular" | custom-call | tf_op jit(solution)/shard_map/jit(cholesky)/cholesky | solution.py:88
  570.9 11.9 %cholesky.490 = f32[128,128]{1,0:T(8,128)S(1)} custom-call(f32[128,128]{1,0:T(8,128)S(1)} %cholesky.597), custom_call_target="Cholesky" | custom-call | tf_op jit(solution)/shard_map/jit(cholesky)/cholesky | solution.py:88
  584.0 9.8 %custom-call.66 = f32[1,128,128]{1,2,0:T(8,128)S(1)} custom-call(f32[1,128,128]{2,1,0:T(8,128)S(1)} %get-tuple-element.39), custom_call_target="InvertDiagBlocksLowerTriangular" | custom-call | tf_op jit(solution)/shard_map/jit(cholesky)/cholesky | solution.py:88
  597.3 11.7 %cholesky.509 = f32[128,128]{1,0:T(8,128)S(1)} custom-call(f32[128,128]{1,0:T(8,128)S(1)} %cholesky.602), custom_call_target="Cholesky" | custom-call | tf_op jit(solution)/shard_map/jit(cholesky)/cholesky | solution.py:88
  610.3 10.0 %custom-call.67 = f32[1,128,128]{1,2,0:T(8,128)S(1)} custom-call(f32[1,128,128]{2,1,0:T(8,128)S(1)} %get-tuple-element.36), custom_call_target="InvertDiagBlocksLowerTriangular" | custom-call | tf_op jit(solution)/shard_map/jit(cholesky)/cholesky | solution.py:88
  623.6 11.7 %cholesky.529 = f32[128,128]{1,0:T(8,128)S(1)} custom-call(f32[128,128]{1,0:T(8,128)S(1)} %cholesky.607), custom_call_target="Cholesky" | custom-call | tf_op jit(solution)/shard_map/jit(cholesky)/cholesky | solution.py:88
  636.6 9.8 %custom-call.68 = f32[1,128,128]{1,2,0:T(8,128)S(1)} custom-call(f32[1,128,128]{2,1,0:T(8,128)S(1)} %get-tuple-element.33), custom_call_target="InvertDiagBlocksLowerTriangular" | custom-call | tf_op jit(solution)/shard_map/jit(cholesky)/cholesky | solution.py:88
  649.4 12.1 %cholesky.549 = f32[128,128]{1,0:T(8,128)S(1)} custom-call(f32[128,128]{1,0:T(8,128)S(1)} %cholesky.612), custom_call_target="Cholesky" | custom-call | tf_op jit(solution)/shard_map/jit(cholesky)/cholesky | solution.py:88
  662.9 9.8 %custom-call.69 = f32[1,128,128]{1,2,0:T(8,128)S(1)} custom-call(f32[1,128,128]{2,1,0:T(8,128)S(1)} %get-tuple-element.30), custom_call_target="InvertDiagBlocksLowerTriangular" | custom-call | tf_op jit(solution)/shard_map/jit(cholesky)/cholesky | solution.py:88
  675.3 11.7 %cholesky.567 = f32[128,128]{1,0:T(8,128)S(1)} custom-call(f32[128,128]{1,0:T(8,128)S(1)} %convolution_subtract_fusion.6), custom_call_target="Cholesky" | custom-call | tf_op jit(solution)/shard_map/jit(cholesky)/cholesky | solution.py:88
  693.3 4.8 select_select_fusion
  698.1 22.8 %while.1 = (s32[]{:T(128)}, f32[1024,1024]{1,0:T(8,128)}, s32[8,2]{0,1:T(2,128)S(1)}, f32[8,128,128]{2,1,0:T(8,128)S(1)}, s32[]{:T(128)}) while((s32[]{:T(128)}, f32[1024,1024]{1,0:T(8,128)}, s32[8,2]{0,1:T(2,128)S(1)}, f32[8,128,128]{2,1,0:T(8,128)S(1)}, s32[]{:T(128)}) %tuple.41), condition=%wide.while_cond, body=%wide.while_body.sunk | while | flops 2 | bytes 131181 | solution.py:89
  721.0 78.8 %custom-call.70 = f32[8,128,128]{1,2,0:T(8,128)S(1)} custom-call(f32[8,128,128]{2,1,0:T(8,128)S(1)} %get-tuple-element.12), custom_call_target="InvertDiagBlocksLowerTriangular" | custom-call | tf_op jit(solution)/shard_map/jit(_solve_triangular)/triangular_solve | solution.py:89
  (132 shorter events, 80.0 us)
Async XLA Ops:
  6.5 130.4 %all-reduce.6.cloned.1.call-start = ((), (), s32[]{:S(2)}) async-start(), calls=%async_computation.1 | async-start | bytes 262144 | tf_op jit(solution)/shard_map/psum | solution.py:80
  11.3 49.7 %copy-start.3 = (s32[1,32]{1,0:T(1,128)S(1)}, s32[1,32]{1,0:T(1,128)}, u32[]{:S(2)}) copy-start(s32[1,32]{1,0:T(1,128)} %param.8) | copy-start | bytes 388
  12.8 10.8 %collective-permute-start = (f32[64,1024]{1,0:T(8,128)S(1)}, f32[64,1024]{1,0:T(8,128)S(1)}, u32[]{:S(2)}, u32[]{:S(2)}) collective-permute-start(f32[64,1024]{1,0:T(8,128)S(1)} %get-tuple-element.25), channel_id=1, source_target_pairs={{0,1},{1,2},{2,3},{3,4},{4,5},{5,6},{6,7},{8,9},{9,10},{10,11},{11... | collective-permute-start | bytes 786440 | tf_op jit(solution)/shard_map/ppermute | solution.py:12
  17.3 7.7 collective-permute-start.1
  25.9 3.8 collective-permute-start.2
  29.8 15.2 %collective-permute-start.3 = (f32[128,1024]{1,0:T(8,128)S(1)}, f32[128,1024]{1,0:T(8,128)S(1)}, u32[]{:S(2)}, u32[]{:S(2)}) collective-permute-start(f32[128,1024]{1,0:T(8,128)S(1)} %add_select_fusion.1), channel_id=1, source_target_pairs={{0,2},{1,3},{2,0},{3,1},{4,6},{5,7},{6,4},{7,5},{8,10},{9,11},{10,... | collective-permute-start | bytes 1572872 | tf_op jit(solution)/shard_map/ppermute | solution.py:18
  45.1 15.9 %collective-permute-start.4 = (f32[128,1024]{1,0:T(8,128)S(1)}, f32[128,1024]{1,0:T(8,128)S(1)}, u32[]{:S(2)}, u32[]{:S(2)}) collective-permute-start(f32[128,1024]{1,0:T(8,128)S(1)} %add_select_fusion), channel_id=1, source_target_pairs={{0,4},{1,5},{2,6},{3,7},{4,0},{5,1},{6,2},{7,3},{8,12},{9,13},{10,... | collective-permute-start | bytes 1572872 | tf_op jit(solution)/shard_map/ppermute | solution.py:18
  62.0 327.6 %reduce-scatter.4.cloned.1.call-start = ((), (), s32[]{:S(2)}) async-start(), calls=%async_computation.3 | async-start | bytes 4259840 | tf_op jit(solution)/shard_map/reduce_scatter | solution.py:81
  143.4 333.9 %all-gather.2.cloned.1.call-start = ((), (), s32[]{:S(2)}) async-start(), calls=%async_computation.2 | async-start | bytes 4259840 | tf_op jit(solution)/shard_map/all_gather | solution.py:87
  487.3 1.9 copy-start
  693.3 106.5 %copy-start.2 = (f32[1024,64]{0,1:T(8,128)S(1)}, f32[1024,64]{0,1:T(8,128)}, u32[]{:S(2)}) copy-start(f32[1024,64]{0,1:T(8,128)} %param.9) | copy-start | bytes 786436
  698.1 112.6 %copy-start.1 = (f32[256,1024]{1,0:T(8,128)S(1)}, f32[256,1024]{1,0:T(8,128)}, u32[]{:S(2)}) copy-start(f32[256,1024]{1,0:T(8,128)} %param.5) | copy-start | bytes 3145732
Sparse Core Ops, SparseCore 0:
  62.2 74.7 all-reduce.5
  143.5 246.1 reduce-scatter.3
  392.7 84.5 all-gather.1
where the time goes:
time: 829 us; the launch traced here: 819 us
  waiting for transfers between devices  436 us (53%)
  other arithmetic  266 us (32%)
  matrix products  43.7 us (5%)
  local copies, waits for them, and re-layouts  32.9 us (4%)
  between operations  20.9 us (3%)
  starting transfers between devices  19.5 us (2%)
    reduce_scatter x1, waiting for transfers between devices, shards(): lax.psum_scatter(jnp.dot(sketch.T, sketch, precision=lax.Precision.HIGHES...  246 us
    another operation x31, other arithmetic, shards(): factor_lower = jnp.linalg.cholesky(gram_matrix)  173 us
    all_gather x1, waiting for transfers between devices, shards(): gram_matrix = lax.all_gather(gram_share, 'dp', axis=0, tiled=True)  87.6 us
    another operation x3, other arithmetic, shards(): jax.scipy.linalg.solve_triangular(factor_lower, gaussian, trans=1, lower=...  83.6 us
    psum x1, waiting for transfers between devices, shards(): sketch = lax.psum(partial_sketch, 'mix')  74.9 us
    ppermute x3, waiting for transfers between devices, partner_2(): return lax.ppermute(value, axis, pairs)  25.5 us
    another operation x14, matrix products, shards(): factor_lower = jnp.linalg.cholesky(gram_matrix)  23.1 us
    another operation x24, local copies, waits for them, and re-layouts  22.7 us
  transfers between devices with their start and end apart: 8, of which 7 were waited for; matrix products, arithmetic and copies ran while one was open for 0% of the time, Pallas kernels for 0%

commit v1 on v0

v1 whole, which is shorter than its diff:
```python
import functools
import math

import jax
import jax.numpy as jnp
from jax import lax
from jax.experimental import pallas as pl
from jax.experimental.pallas import tpu as pltpu
from jax.sharding import PartitionSpec as P

HI = lax.Precision.HIGHEST
NN = (((1,), (0,)), ((), ()))
NT = (((1,), (1,)), ((), ()))
TN = (((0,), (0,)), ((), ()))
MESH = pl.DeviceIdType.MESH


def gram_kernel(n_mix, n, hs_ref, x_ref, g_ref, part, r1, s_all, w, r3, q, r4, f, *sems):
    (s1, v1, s2, v2, s3, v3, s4, v4, s5, v5, s6, v6, s7, v7, local) = sems
    dp, m = lax.axis_index("dp"), lax.axis_index("mix")
    y, z = dp // n, dp % n
    core = m % 2
    n_off = n_mix // 2 + 1
    piece = 128 // (2 * n)

    def mix_peer(d):
        return (dp, (m + d) % n_mix)

    def y_peer(d):
        return (((y + d) % n) * n + z, m)

    def z_peer(d):
        return (y * n + (z + d) % n, m)

    barrier = pltpu.get_barrier_semaphore()
    for d in range(1, n_mix):
        pl.semaphore_signal(barrier, inc=1, device_id=mix_peer(d), device_id_type=MESH)
    for d in range(1, n):
        pl.semaphore_signal(barrier, inc=1, device_id=y_peer(d), device_id_type=MESH)
        pl.semaphore_signal(barrier, inc=1, device_id=z_peer(d), device_id_type=MESH)

    def send(src, dst, ssem, rsem, peer):
        copy = pltpu.make_async_remote_copy(src_ref=src, dst_ref=dst, send_sem=ssem, recv_sem=rsem,
                                            device_id=peer, device_id_type=MESH)
        copy.start()
        return copy

    product = lax.dot_general(hs_ref[...], x_ref[...], NN, precision=HI, preferred_element_type=jnp.float32)
    product = product * (1.0 / math.sqrt(n_mix * 128 * hs_ref.shape[0]))
    for b in range(n_mix):
        part[b] = product[:, 128 * b:128 * b + 128]
    pl.semaphore_wait(barrier, n_mix - 1 + 2 * (n - 1))
    sent = []

    got = []
    for d in range(1, n_mix):
        p = (m + d) % n_mix
        got.append(send(part.at[p], r1.at[m], s1.at[d], v1.at[d], mix_peer(d)))
    r1[m] = part[m]
    for copy in got:
        copy.wait_recv()
    sent += got
    s_all[m] = functools.reduce(jnp.add, [r1[b] for b in range(n_mix)])
    got = []
    for d in range(1, n_mix):
        got.append(send(s_all.at[m], s_all.at[m], s2.at[d], v2.at[d], mix_peer(d)))
    for copy in got:
        copy.wait_recv()
    sent += got

    for o in range(n_off):
        b = (m + o) % n_mix
        low, high = jnp.minimum(m, b), jnp.maximum(m, b)
        tile = lax.dot_general(s_all[high], s_all[low], TN, precision=HI, preferred_element_type=jnp.float32)
        for h in range(2):
            for p in range(n):
                r = (h * n + p) * piece
                w[h, p, o] = tile[r:r + piece]

    got = []
    for d in range(1, n):
        got.append(send(w.at[0, (y + d) % n], r3.at[0, y], s3.at[0, d], v3.at[0, d], y_peer(d)))
        got.append(send(w.at[1, (z + d) % n], r3.at[1, z], s3.at[1, d], v3.at[1, d], z_peer(d)))
    r3[0, y] = w[0, y]
    r3[1, z] = w[1, z]
    for copy in got:
        copy.wait_recv()
    sent += got
    for h in range(2):
        q[h] = functools.reduce(jnp.add, [r3[h, p] for p in range(n)])
    got = []
    for d in range(1, n):
        got.append(send(q.at[0], r4.at[0, z], s4.at[0, d], v4.at[0, d], z_peer(d)))
        got.append(send(q.at[1], r4.at[1, y], s4.at[1, d], v4.at[1, d], y_peer(d)))
    r4[0, z] = q[0]
    r4[1, y] = q[1]
    for copy in got:
        copy.wait_recv()
    sent += got
    for h in range(2):
        f[h, m] = functools.reduce(jnp.add, [r4[h, p] for p in range(n)])

    got = []
    for d in range(1, n_mix):
        for h in range(2):
            got.append(send(f.at[h, m], f.at[h, m], s5.at[h, d], v5.at[h, d], mix_peer(d)))
    for copy in got:
        copy.wait_recv()
    sent += got
    place = y + core * (z - y)
    sibling = (dp, m + 1 - 2 * core)
    got = []
    for d in range(1, n):
        peer = (((y + d * (1 - core)) % n) * n + (z + d * core) % n, m)
        got.append(send(f.at[core], g_ref.at[core, place], s6.at[d], v6.at[d], peer))
    own = pltpu.make_async_copy(f.at[core], g_ref.at[core, place], local)
    own.start()
    across = [send(f.at[core], g_ref.at[core, place], s7.at[0], v7.at[0], sibling)]
    for d in range(1, n):
        got[d - 1].wait_recv()
        slot = (place + n - d) % n
        across.append(send(g_ref.at[core, slot], g_ref.at[core, slot], s7.at[d], v7.at[d], sibling))
    sent += got + across
    own.wait()
    for copy in across:
        copy.wait_recv()
    for copy in sent:
        copy.wait_send()


def gram_call(n_mix, n, hs, x):
    vm = pl.BlockSpec(memory_space=pltpu.VMEM)
    n_off, piece, k = n_mix // 2 + 1, 128 // (2 * n), hs.shape[0]
    f32 = jnp.float32
    dma = pltpu.SemaphoreType.DMA
    pair = lambda *s: [dma(s), dma(s)]
    return pl.pallas_call(
        functools.partial(gram_kernel, n_mix, n),
        out_shape=jax.ShapeDtypeStruct((2, n, n_mix, n_off, piece, 128), f32),
        in_specs=[vm] * 2, out_specs=vm,
        scratch_shapes=[
            pltpu.VMEM((n_mix, k, 128), f32), pltpu.VMEM((n_mix, k, 128), f32), pltpu.VMEM((n_mix, k, 128), f32),
            pltpu.VMEM((2, n, n_off, piece, 128), f32), pltpu.VMEM((2, n, n_off, piece, 128), f32),
            pltpu.VMEM((2, n_off, piece, 128), f32), pltpu.VMEM((2, n, n_off, piece, 128), f32),
            pltpu.VMEM((2, n_mix, n_off, piece, 128), f32),
            *pair(n_mix), *pair(n_mix), *pair(2, n), *pair(2, n), *pair(2, n_mix), *pair(n), *pair(n), dma(())],
        compiler_params=pltpu.CompilerParams(collective_id=0, has_side_effects=True, vmem_limit_bytes=32 * 1024 * 1024),
    )(hs, x)


def mm(a, b, dims):
    return lax.dot_general(a, b, dims, precision=HI, preferred_element_type=jnp.float32)


def factor_inverse(d_ref, t_ref):
    shape = (8, 128)
    lane = lax.broadcasted_iota(jnp.int32, shape, 1)
    sub = lax.broadcasted_iota(jnp.int32, shape, 0)
    tiles = [d_ref[8 * t:8 * t + 8, :] for t in range(16)]
    lanes_of = lambda x, c: jnp.broadcast_to(x[:, c:c + 1], shape)
    rows_of = lambda x, r: jnp.broadcast_to(x[r:r + 1, :], shape)
    for t in range(16):
        base = 8 * t
        own = tiles[t]
        cols = [lanes_of(own, base + j) for j in range(8)]
        e = [[rows_of(cols[j], i) for j in range(i + 1)] for i in range(8)]
        row = [rows_of(own, i) for i in range(8)]
        piv, inv, low = [], [], {}
        for k in range(8):
            piv.append(e[k][k])
            inv.append(1.0 / e[k][k])
            for i in range(k + 1, 8):
                low[i, k] = e[i][k] * inv[k]
            for i in range(k + 1, 8):
                for j in range(k + 1, i + 1):
                    e[i][j] = e[i][j] - low[i, k] * e[j][k]
        tri = {}
        for i in range(8):
            for j in range(i):
                acc = low[i, j]
                for k in range(j + 1, i):
                    acc = acc + low[i, k] * tri[k, j]
                tri[i, j] = -acc
        inside = (lane >= base) & (lane < base + 8)
        rows = []
        for i in range(8):
            acc = row[i]
            patt = jnp.where(lane == base + i, 1.0, 0.0)
            for k in range(i):
                acc = acc + tri[i, k] * row[k]
                patt = jnp.where(lane == base + k, tri[i, k], patt)
            rows.append(jnp.where(inside, patt, acc))
        out = jnp.zeros(shape, jnp.float32)
        for i in range(8):
            out = jnp.where(sub == i, rows[i] * lax.rsqrt(piv[i]), out)
        t_ref[base:base + 8, :] = jnp.where(lane <= base + sub, out, 0.0)
        scaled = [rows[k] * inv[k] for k in range(8)]
        for u in range(t + 1, 16):
            c0 = [lanes_of(tiles[u], base + j) for j in range(8)]
            acc = jnp.where(inside, 0.0, tiles[u])
            for k in range(8):
                c = c0[k]
                for j in range(k):
                    c = c + tri[k, j] * c0[j]
                acc = acc - c * scaled[k]
            tiles[u] = acc


def chol_kernel(g_ref, gt_ref, x_ref, keep_ref, o_ref, a_ref, t_ref, y_ref, d_ref, acc_ref, xt_ref):
    nb = 8
    for i in range(nb):
        for j in range(i + 1):
            m, o = (j, i - j) if i - j <= 4 else (i, 8 - i + j)
            for h in range(2):
                for p in range(8):
                    r = i * 128 + h * 64 + p * 8
                    a_ref[r:r + 8, j * 128:j * 128 + 128] = g_ref[h, p, m, o]
    y_ref[...] = jnp.zeros_like(y_ref)

    def step(kb, carry):
        at = pl.multiple_of(kb * 128, 128)
        d_ref[...] = a_ref[pl.ds(at, 128), pl.ds(at, 128)]
        factor_inverse(d_ref, t_ref.at[kb])
        tri = t_ref[kb]
        for c in range(nb):
            @pl.when(kb == c)
            def _():
                if c:
                    y_ref[128 * c:128 * c + 128, :128 * c] = mm(tri, a_ref[128 * c:128 * c + 128, :128 * c], NN)
                if c < nb - 1:
                    lo = 128 * (c + 1)
                    for i in range(c + 1, nb):
                        a_ref[128 * i:128 * i + 128, 128 * c:lo] = mm(a_ref[128 * i:128 * i + 128, 128 * c:lo], tri, NT)
                    for i in range(c + 1, nb):
                        hi = 128 * (i + 1)
                        v = a_ref[128 * i:hi, 128 * c:lo]
                        a_ref[128 * i:hi, lo:hi] = a_ref[128 * i:hi, lo:hi] - mm(v, a_ref[lo:hi, 128 * c:lo], NT)
        return carry

    lax.fori_loop(0, nb, step, 0)
    acc_ref[...] = gt_ref[...]
    for i in range(nb - 1, -1, -1):
        s = slice(128 * i, 128 * i + 128)
        head = acc_ref[:, s]
        xt_ref[:, s] = mm(head, t_ref[i], NN)
        if i:
            acc_ref[:, :128 * i] = acc_ref[:, :128 * i] - mm(head, y_ref[s, :128 * i], NN)
    proj = mm(xt_ref[...], x_ref[...], NT)
    o_ref[...] = jnp.where(keep_ref[...] > 0, jnp.sum(proj * proj, axis=0, keepdims=True), 0.0)


def chol_call(g, gt, x, keep):
    vm = pl.BlockSpec(memory_space=pltpu.VMEM)
    return pl.pallas_call(
        chol_kernel,
        out_shape=jax.ShapeDtypeStruct((1, 256), jnp.float32),
        in_specs=[vm] * 4, out_specs=vm,
        scratch_shapes=[pltpu.VMEM((1024, 1024), jnp.float32), pltpu.VMEM((8, 128, 128), jnp.float32),
                        pltpu.VMEM((1024, 1024), jnp.float32), pltpu.VMEM((128, 128), jnp.float32),
                        pltpu.VMEM((64, 1024), jnp.float32), pltpu.VMEM((64, 1024), jnp.float32)],
        compiler_params=pltpu.CompilerParams(vmem_limit_bytes=48 * 1024 * 1024),
    )(g, gt, x, keep)


def shards(matrix, counts, sign_bits, samples, gaussian):
    capacity = matrix.shape[0]
    n_mix, n_dp = lax.axis_size("mix"), lax.axis_size("dp")
    mix_index = lax.axis_index("mix")
    member = jnp.arange(n_mix, dtype=jnp.int32)
    first_row = jnp.sum(jnp.where(member < mix_index, counts[0], 0))
    own_count = jnp.sum(jnp.where(member == mix_index, counts[0], 0))
    slots = jnp.arange(capacity, dtype=jnp.int32)
    kept = slots < own_count
    common = jnp.bitwise_and(samples[0][:, None], (first_row + slots)[None, :])
    odd = jnp.bitwise_and(lax.population_count(common), 1)
    signs = (1 - 2 * odd) * (2 * sign_bits - 1)[None, :]
    table = jnp.where(kept[None, :], signs, 0).astype(jnp.float32)
    grams = gram_call(n_mix, math.isqrt(n_dp), table, matrix)
    keep = kept.astype(jnp.int32)[None, :]
    return chol_call(grams, gaussian.T, matrix, keep)[0]


def solution(mesh):
    in_specs = (P(("dp", "mix"), None), P("dp", None), P(("dp", "mix")), P("dp", None), P())
    out_specs = P(("dp", "mix"))
    return jax.shard_map(shards, mesh=mesh, in_specs=in_specs, out_specs=out_specs, check_vma=False)
```

time: 829 us -> 125 us (0.15); the launches traced: 819 us -> 124 us
  waiting for transfers between devices: 436 us -> 0 us
  other arithmetic: 266 us -> 4.79 us
  Pallas kernels: 0 us -> 118 us
  matrix products: 43.7 us -> 0 us
  local copies, waits for them, and re-layouts: 32.9 us -> 1.23 us
  between operations: 20.9 us -> 0.05 us
  starting transfers between devices: 19.5 us -> 0 us
    another operation x34 -> x0, other arithmetic: 257 us -> none  [the longest x31 173 us: shards(): factor_lower = jnp.linalg.cholesky(gram_matrix)]
    reduce_scatter x1 -> x0, waiting for transfers between devices: 246 us -> none  [shards(): lax.psum_scatter(jnp.dot(sketch.T, sketch, precision=lax.Precision.HIGHES...]
    pallas_call x0 -> x2, Pallas kernels: none -> 118 us  [the longest x1 64.2 us: gram_call(): pl.pallas_call(functools.partial(gram_kernel, n_mix, n), out_shape=jax.Sh...]
    all_gather x1 -> x0, waiting for transfers between devices: 87.6 us -> none  [shards(): gram_matrix = lax.all_gather(gram_share, 'dp', axis=0, tiled=True)]
    psum x1 -> x0, waiting for transfers between devices: 74.9 us -> none  [shards(): sketch = lax.psum(partial_sketch, 'mix')]
    another operation x29 -> x0, matrix products: 33.7 us -> none  [the longest x14 23.1 us: shards(): factor_lower = jnp.linalg.cholesky(gram_matrix)]
    ppermute x5 -> x0, waiting for transfers between devices: 26.9 us -> none  [the longest x3 25.5 us: partner_2(): return lax.ppermute(value, axis, pairs)]
    another operation x37 -> x0, local copies, waits for them, and re-layouts: 25.3 us -> none
  transfers between devices with their start and end apart: 8 -> 0, of which waited for: 7 -> 0; matrix products, arithmetic and copies ran while one was open for 0% -> 0% of each run, Pallas kernels for 0% -> 0%
where the time goes in v1:
time: 125 us; the launch traced here: 124 us
  Pallas kernels  118 us (94%)
  other arithmetic  4.79 us (4%)
    pallas_call x1, Pallas kernels, gram_call(): pl.pallas_call(functools.partial(gram_kernel, n_mix, n), out_shape=jax.Sh...  64.2 us
    pallas_call x1, Pallas kernels, chol_call(): pl.pallas_call(chol_kernel, out_shape=jax.ShapeDtypeStruct((1, 256), jnp....  54.1 us

profile of v1, /device:TPU:1, one launch (start us, length us, event | category | flops | bytes accessed | tf_op | source)
XLA Modules:
  0.0 124.4 jit_solution(4020340321847196819)
XLA Ops:
  0.0 1.4 %fusion = (s32[]{:T(128)}, s32[]{:T(128)}) fusion(s32[1,8]{1,0:T(1,128)} %param.6, s32[]{:T(128)S(6)} %axis_index.12), kind=kLoop, calls=%fused_computation.7 | loop fusion | flops 46 | bytes 44 | tf_op jit(solution)/shard_map/reduce_sum | solution.py:271
  1.4 1.4 %multiply_add_fusion = (s32[256]{0:T(256)S(1)}, s32[256]{0:T(256)S(1)}) fusion(s32[256]{0:T(256)} %param.7, s32[]{:T(128)} %get-tuple-element.6), kind=kLoop, calls=%fused_computation.4 | loop fusion | flops 768 | bytes 3076 | tf_op jit(solution)/shard_map/sub | solution.py:276
  2.7 0.6 iota_compare_fusion
  3.4 0.7 select_convert_fusion.hs_ref
  4.1 0.0 copy-start
  4.2 1.2 copy-done
  5.4 0.0 copy-start.1
  5.4 0.0 copy-start.2
  5.4 64.2 %shard_map.55.g_ref = f32[2,8,8,5,8,128]{5,4,3,2,1,0:T(8,128)S(1)} custom-call(f32[32,256]{1,0:T(8,128)S(1)} %select_convert_fusion.hs_ref, f32[256,1024]{1,0:T(8,128)S(1)} %copy-done), custom_call_target="tpu_custom_call" | custom-call | tf_op jit(solution)/shard_map/pallas_call | solution.py:137
  69.5 0.7 compare_convert_fusion.keep_ref
  70.2 0.0 copy-done.1
  70.2 0.0 copy-done.2
  70.2 54.1 %shard_map.56 = f32[1,256]{1,0:T(1,128)} custom-call(f32[2,8,8,5,8,128]{5,4,3,2,1,0:T(8,128)S(1)} %shard_map.55.g_ref, f32[64,1024]{1,0:T(8,128)S(1)} %bitcast.6, f32[256,1024]{1,0:T(8,128)S(1)} %copy-done.1, s32[1,256]{1,0:T(1,128)S(1)} %compare_convert_fusion.keep_ref), custom_call_target="tpu_custom_call" | custom-call | tf_op jit(solution)/shard_map/pallas_call | solution.py:254
Async XLA Ops:
  4.1 1.2 copy-start
  5.4 64.8 %copy-start.1 = (f32[256,1024]{1,0:T(8,128)S(1)}, f32[256,1024]{1,0:T(8,128)}, u32[]{:S(2)}) copy-start(f32[256,1024]{1,0:T(8,128)} %x_ref.3) | copy-start | bytes 3145732
  5.4 64.8 %copy-start.2 = (f32[1024,64]{0,1:T(8,128)S(1)}, f32[1024,64]{0,1:T(8,128)}, u32[]{:S(2)}) copy-start(f32[1024,64]{0,1:T(8,128)} %param.9) | copy-start | bytes 786436

commit v2 on v1

v2 whole, which is shorter than its diff:
```python
import functools
import math

import jax
import jax.numpy as jnp
from jax import lax
from jax.experimental import pallas as pl
from jax.experimental.pallas import tpu as pltpu
from jax.sharding import PartitionSpec as P

HI = lax.Precision.HIGHEST
NN = (((1,), (0,)), ((), ()))
NT = (((1,), (1,)), ((), ()))
TN = (((0,), (0,)), ((), ()))
MESH = pl.DeviceIdType.MESH
CHUNKS = 4


def own_rows(counts_ref, n_mix):
    m = lax.axis_index("mix")
    first, count = jnp.int32(0), jnp.int32(0)
    for i in range(n_mix):
        first = first + jnp.where(i < m, counts_ref[0, i], 0)
        count = count + jnp.where(i == m, counts_ref[0, i], 0)
    return first, count


def gram_kernel(n_mix, n, counts_ref, samples_ref, bits_ref, x_ref, g_ref,
                part, r1, s_all, w, r3, q, r4, f, *sems):
    (s1, v1, s2, v2, s3, v3, s4, v4, s5, v5, s6, v6, s7, v7, local) = sems
    dp, m = lax.axis_index("dp"), lax.axis_index("mix")
    y, z = dp // n, dp % n
    x, core = m // 2, m % 2
    nx = n_mix // 2
    n_off = n_mix // 2 + 1
    piece = 128 // (2 * n)
    capacity, picks = x_ref.shape[0], samples_ref.shape[1]

    def mix_peer(d):
        return (dp, (m + d) % n_mix)

    def y_peer(d):
        return (((y + d) % n) * n + z, m)

    def z_peer(d):
        return (y * n + (z + d) % n, m)

    barrier = pltpu.get_barrier_semaphore()
    for d in range(1, n_mix):
        pl.semaphore_signal(barrier, inc=1, device_id=mix_peer(d), device_id_type=MESH)
    for d in range(1, n):
        pl.semaphore_signal(barrier, inc=1, device_id=y_peer(d), device_id_type=MESH)
        pl.semaphore_signal(barrier, inc=1, device_id=z_peer(d), device_id_type=MESH)

    def send(src, dst, ssem, rsem, peer):
        copy = pltpu.make_async_remote_copy(src_ref=src, dst_ref=dst, send_sem=ssem, recv_sem=rsem,
                                            device_id=peer, device_id_type=MESH)
        copy.start()
        return copy

    first, count = own_rows(counts_ref, n_mix)
    slot = lax.broadcasted_iota(jnp.int32, (8, capacity), 1)
    row = lax.broadcasted_iota(jnp.int32, (8, capacity), 0)
    sign = jnp.where(slot < count, 2 * bits_ref[...] - 1, 0)
    table = []
    for base in range(0, picks, 8):
        sample = jnp.zeros((8, capacity), jnp.int32)
        for i in range(8):
            sample = jnp.where(row == i, samples_ref[0, base + i], sample)
        odd = jnp.bitwise_and(sample, first + slot)
        for shift in (8, 4, 2, 1):
            odd = jnp.bitwise_xor(odd, jnp.right_shift(odd, shift))
        table.append(jnp.where(jnp.bitwise_and(odd, 1) == 1, -sign, sign))
    table = jnp.concatenate(table, axis=0).astype(jnp.float32).astype(jnp.bfloat16)
    scale = 1.0 / math.sqrt(n_mix * 128 * picks)
    for b in range(n_mix):
        rest = x_ref[:, 128 * b:128 * b + 128]
        total = None
        for _ in range(3):
            term = rest.astype(jnp.bfloat16)
            rest = rest - term.astype(jnp.float32)
            product = lax.dot_general(table, term, NN, preferred_element_type=jnp.float32)
            total = product if total is None else total + product
        part[b] = total * scale
    pl.semaphore_wait(barrier, n_mix - 1 + 2 * (n - 1))
    sent = []

    got = []
    for d in range(1, n_mix):
        p = (m + d) % n_mix
        got.append(send(part.at[p], r1.at[m], s1.at[d], v1.at[d], mix_peer(d)))
    r1[m] = part[m]
    for copy in got:
        copy.wait_recv()
    sent += got
    s_all[m] = functools.reduce(jnp.add, [r1[b] for b in range(n_mix)])
    got = []
    for d in range(1, n_mix):
        got.append(send(s_all.at[m], s_all.at[m], s2.at[d], v2.at[d], mix_peer(d)))
    for copy in got:
        copy.wait_recv()
    sent += got

    for o in range(n_off):
        b = (m + o) % n_mix
        low, high = jnp.minimum(m, b), jnp.maximum(m, b)
        tile = lax.dot_general(s_all[high], s_all[low], TN, precision=HI, preferred_element_type=jnp.float32)
        for h in range(2):
            for p in range(n):
                r = (h * n + p) * piece
                w[h, p, o] = tile[r:r + piece]

    got = []
    for d in range(1, n):
        got.append(send(w.at[0, (y + d) % n], r3.at[0, y], s3.at[0, d], v3.at[0, d], y_peer(d)))
        got.append(send(w.at[1, (z + d) % n], r3.at[1, z], s3.at[1, d], v3.at[1, d], z_peer(d)))
    r3[0, y] = w[0, y]
    r3[1, z] = w[1, z]
    for copy in got:
        copy.wait_recv()
    sent += got
    for h in range(2):
        q[h] = functools.reduce(jnp.add, [r3[h, p] for p in range(n)])
    got = []
    for d in range(1, n):
        got.append(send(q.at[0], r4.at[0, z], s4.at[0, d], v4.at[0, d], z_peer(d)))
        got.append(send(q.at[1], r4.at[1, y], s4.at[1, d], v4.at[1, d], y_peer(d)))
    r4[0, z] = q[0]
    r4[1, y] = q[1]
    for copy in got:
        copy.wait_recv()
    sent += got
    for h in range(2):
        f[h, m] = functools.reduce(jnp.add, [r4[h, p] for p in range(n)])

    got = []
    for d in range(nx):
        column = ((x + d) % nx) * 2
        if d:
            got.append(send(f.at[core, m], f.at[core, m], s5.at[0, d], v5.at[0, d], (dp, column + core)))
        got.append(send(f.at[1 - core, m], f.at[1 - core, m], s5.at[1, d], v5.at[1, d], (dp, column + 1 - core)))
    for copy in got:
        copy.wait_recv()
    sent += got

    place = y + core * (z - y)
    sibling = (dp, m + 1 - 2 * core)
    up = (((y + 1 - core) % n) * n + (z + core) % n, m)
    down = (((y + n - 1 + core) % n) * n + (z + n - core) % n, m)
    width = n_mix // CHUNKS
    far = n // 2
    own = pltpu.make_async_copy(f.at[core], g_ref.at[core, place], local)
    own.start()

    def relay(way, d, c, source):
        at = (place + (n - d if way == 0 else d)) % n
        rows = pl.ds(c * width, width)
        dst = g_ref.at[core, at, rows]
        return send(source if d == 0 else dst, dst, s6.at[way, d, c], v6.at[way, d, c], (up, down)[way])

    def goes(way, d, c):
        return d < far - 1 or (d == far - 1 and (c < CHUNKS // 2) == (way == 0))

    moves = {}
    across = []
    for c in range(CHUNKS):
        for way in range(2):
            if goes(way, 0, c):
                moves[way, 0, c] = relay(way, 0, c, f.at[core, pl.ds(c * width, width)])
    across.append(send(f.at[core], g_ref.at[core, place], s7.at[0, 0, 0], v7.at[0, 0, 0], sibling))
    for d in range(1, far + 1):
        for c in range(CHUNKS):
            for way in range(2):
                if goes(way, d - 1, c):
                    moves[way, d - 1, c].wait_recv()
                    if goes(way, d, c):
                        moves[way, d, c] = relay(way, d, c, None)
                    at = (place + (n - d if way == 0 else d)) % n
                    block = g_ref.at[core, at, pl.ds(c * width, width)]
                    across.append(send(block, block, s7.at[way, d, c], v7.at[way, d, c], sibling))
    own.wait()
    for copy in across:
        copy.wait_recv()
    for copy in sent + across + list(moves.values()):
        copy.wait_send()


def gram_call(n_mix, n, counts, samples, bits, x):
    vm = pl.BlockSpec(memory_space=pltpu.VMEM)
    sm = pl.BlockSpec(memory_space=pltpu.SMEM)
    n_off, piece, k = n_mix // 2 + 1, 128 // (2 * n), samples.shape[1]
    f32 = jnp.float32
    dma = pltpu.SemaphoreType.DMA
    pair = lambda *s: [dma(s), dma(s)]
    return pl.pallas_call(
        functools.partial(gram_kernel, n_mix, n),
        out_shape=jax.ShapeDtypeStruct((2, n, n_mix, n_off, piece, 128), f32),
        in_specs=[sm, sm, vm, vm], out_specs=vm,
        scratch_shapes=[
            pltpu.VMEM((n_mix, k, 128), f32), pltpu.VMEM((n_mix, k, 128), f32), pltpu.VMEM((n_mix, k, 128), f32),
            pltpu.VMEM((2, n, n_off, piece, 128), f32), pltpu.VMEM((2, n, n_off, piece, 128), f32),
            pltpu.VMEM((2, n_off, piece, 128), f32), pltpu.VMEM((2, n, n_off, piece, 128), f32),
            pltpu.VMEM((2, n_mix, n_off, piece, 128), f32),
            *pair(n_mix), *pair(n_mix), *pair(2, n), *pair(2, n), *pair(2, n_mix // 2),
            *pair(2, n // 2 + 1, CHUNKS), *pair(2, n // 2 + 1, CHUNKS), dma(())],
        compiler_params=pltpu.CompilerParams(collective_id=0, has_side_effects=True, vmem_limit_bytes=32 * 1024 * 1024),
    )(counts, samples, bits, x)


def mm(a, b, dims):
    return lax.dot_general(a, b, dims, precision=HI, preferred_element_type=jnp.float32)


def split(x):
    high = x.astype(jnp.bfloat16)
    rest = x - high.astype(jnp.float32)
    mid = rest.astype(jnp.bfloat16)
    return high, mid, (rest - mid.astype(jnp.float32)).astype(jnp.bfloat16)


def left_terms(x):
    high, mid, low = split(x)
    return jnp.concatenate([high, high, mid, high, low, mid], axis=1)


def right_terms(x):
    high, mid, low = split(x)
    return jnp.concatenate([high, mid, high, low, high, mid], axis=1)


def wide(a, b):
    return lax.dot_general(a, b, NT, preferred_element_type=jnp.float32)


def mm3(a, b, dims):
    ah, bh = a.astype(jnp.bfloat16), b.astype(jnp.bfloat16)
    al = (a - ah.astype(jnp.float32)).astype(jnp.bfloat16)
    bl = (b - bh.astype(jnp.float32)).astype(jnp.bfloat16)
    dot = functools.partial(lax.dot_general, dimension_numbers=dims, preferred_element_type=jnp.float32)
    return dot(ah, bh) + (dot(ah, bl) + dot(al, bh))


def factor_inverse(d_ref, t_ref, zero):
    shape = (8, 128)
    lane = lax.broadcasted_iota(jnp.int32, shape, 1)
    sub = lax.broadcasted_iota(jnp.int32, shape, 0)
    tiles = [d_ref[8 * t:8 * t + 8, :] for t in range(16)]
    lanes_of = lambda x, c: jnp.broadcast_to(x[:, c:c + 1], shape)
    rows_of = lambda x, r: jnp.broadcast_to(x[r:r + 1, :], shape)
    cols = [lanes_of(tiles[0], j) + zero for j in range(8)]
    for t in range(16):
        base = 8 * t
        inside = (lane >= base) & (lane < base + 8)
        below = [[lanes_of(tiles[u], base + j) for j in range(8)] for u in range(t + 1, 16)]
        if t < 15:
            x = [b + zero for b in below[0]]
            ahead = [lanes_of(tiles[t + 1], base + 8 + j) + zero for j in range(8)]
        row = jnp.where(inside, jnp.where(lane == base + sub, 1.0, 0.0), tiles[t])
        low, inv_col, piv_col = {}, zero, zero + 1.0
        for k in range(8):
            pivot = rows_of(cols[k], k)
            inv = 1.0 / pivot
            factor = cols[k] * inv
            for j in range(k + 1, 8):
                cols[j] = cols[j] - factor * rows_of(cols[k], j)
                low[j, k] = rows_of(factor, j)
            inv_col = jnp.where(sub == k, inv, inv_col)
            piv_col = jnp.where(sub == k, pivot, piv_col)
            if k < 7:
                row = row - jnp.where(sub > k, factor, 0.0) * rows_of(row, k)
            if t < 15:
                y = x[k] * inv
                ahead = [ahead[j] - y * rows_of(x[k], j) for j in range(8)]
                for i in range(k + 1, 8):
                    x[i] = x[i] - low[i, k] * x[k]
        t_ref[base:base + 8, :] = jnp.where(lane <= base + sub, row * lax.rsqrt(piv_col), 0.0)
        if t == 15:
            break
        cols = ahead
        row = row * inv_col
        solved = [rows_of(row, k) for k in range(8)]
        for k in range(7, 0, -1):
            for j in range(k):
                solved[j] = solved[j] - low[k, j] * solved[k]
        for u in range(t + 1, 16):
            acc = jnp.where(inside, 0.0, tiles[u])
            for k in range(8):
                acc = acc - below[u - t - 1][k] * solved[k]
            tiles[u] = acc


def chol_kernel(counts_ref, g_ref, gt_ref, x_ref, o_ref, a_ref, tp_ref, t_ref, d_ref, acc_ref, xt_ref, tr_ref, vl_ref, vr_ref, z_ref):
    nb = 8
    size = 128 * nb
    for i in range(nb):
        for j in range(i + 1):
            m, o = (j, i - j) if i - j <= 4 else (i, 8 - i + j)
            for h in range(2):
                for p in range(8):
                    r = i * 128 + h * 64 + p * 8
                    a_ref[r:r + 8, j * 128:j * 128 + 128] = g_ref[h, p, m, o]
    for i in range(1, nb, 2):
        a_ref[128 * i - 128:128 * i, 128 * i:128 * i + 128] = jnp.zeros((128, 128), jnp.float32)
    z_ref[...] = jnp.zeros_like(z_ref)
    tr_ref[...] = jnp.zeros_like(tr_ref)
    tp_ref[...] = jnp.zeros_like(tp_ref)
    d_ref[...] = a_ref[:128, :128]

    def step(kb, carry):
        past = pl.multiple_of(jnp.maximum(kb - 1, 0) * 128, 128)
        here = pl.multiple_of(kb * 128, 128)
        col = a_ref[:, pl.ds(past, 128)]
        row_ids = lax.broadcasted_iota(jnp.int32, (size, 128), 0)
        mine = (row_ids >= here) & (kb > 0)
        v = jnp.where(mine, wide(left_terms(col), tr_ref[...]), 0.0)
        a_ref[:, pl.ds(past, 128)] = jnp.where(mine, v, col)
        vl_ref[...] = left_terms(v)
        vr_ref[...] = right_terms(v)
        for left in range(0, size, 256):
            part = wide(vl_ref[left:, :], vr_ref[left:left + 256, :])
            a_ref[left:, left:left + 256] = a_ref[left:, left:left + 256] - part
        factor_inverse(d_ref, t_ref, z_ref[...])
        tri = t_ref[...]
        half = pl.multiple_of((kb % 2) * 128, 128)
        tp_ref[kb // 2, pl.ds(half, 128), pl.ds(half, 128)] = tri
        right = right_terms(tri)
        tr_ref[...] = right
        then = pl.multiple_of(jnp.minimum(kb + 1, nb - 1) * 128, 128)
        v = wide(left_terms(a_ref[pl.ds(then, 128), pl.ds(here, 128)]), right)
        d_ref[...] = a_ref[pl.ds(then, 128), pl.ds(then, 128)] - wide(left_terms(v), right_terms(v))
        return carry

    lax.fori_loop(0, nb, step, 0)
    for q in range(nb // 2):
        s = 256 * q
        link = mm3(a_ref[s + 128:s + 256, s:s + 128], tp_ref[q, :128, :128], NN)
        tp_ref[q, 128:, :128] = -mm3(tp_ref[q, 128:, 128:], link, NN)
    acc_ref[...] = gt_ref[...]
    for q in range(nb // 2 - 1, -1, -1):
        s = slice(256 * q, 256 * q + 256)
        part = mm3(acc_ref[:, s], tp_ref[q], NN)
        xt_ref[:, s] = part
        if q:
            acc_ref[:, :256 * q] = acc_ref[:, :256 * q] - mm3(part, a_ref[s, :256 * q], NN)
    proj = mm3(xt_ref[...], x_ref[...], NT)
    _, count = own_rows(counts_ref, counts_ref.shape[1])
    slot = lax.broadcasted_iota(jnp.int32, o_ref.shape, 1)
    o_ref[...] = jnp.where(slot < count, jnp.sum(proj * proj, axis=0, keepdims=True), 0.0)


def chol_call(counts, g, gt, x):
    vm = pl.BlockSpec(memory_space=pltpu.VMEM)
    f32, bf16 = jnp.float32, jnp.bfloat16
    return pl.pallas_call(
        chol_kernel,
        out_shape=jax.ShapeDtypeStruct((1, 256), f32),
        in_specs=[pl.BlockSpec(memory_space=pltpu.SMEM)] + [vm] * 3, out_specs=vm,
        scratch_shapes=[pltpu.VMEM((1024, 1024), f32), pltpu.VMEM((4, 256, 256), f32), pltpu.VMEM((128, 128), f32),
                        pltpu.VMEM((128, 128), f32), pltpu.VMEM((64, 1024), f32), pltpu.VMEM((64, 1024), f32),
                        pltpu.VMEM((128, 768), bf16), pltpu.VMEM((1024, 768), bf16), pltpu.VMEM((1024, 768), bf16),
                        pltpu.VMEM((8, 128), f32)],
        compiler_params=pltpu.CompilerParams(vmem_limit_bytes=48 * 1024 * 1024),
    )(counts, g, gt, x)


def shards(matrix, counts, sign_bits, samples, gaussian):
    n_mix, n_dp = lax.axis_size("mix"), lax.axis_size("dp")
    grams = gram_call(n_mix, math.isqrt(n_dp), counts, samples, sign_bits[None, :], matrix)
    return chol_call(counts, grams, gaussian.T, matrix)[0]


def solution(mesh):
    in_specs = (P(("dp", "mix"), None), P("dp", None), P(("dp", "mix")), P("dp", None), P())
    out_specs = P(("dp", "mix"))
    return jax.shard_map(shards, mesh=mesh, in_specs=in_specs, out_specs=out_specs, check_vma=False)
```

time: 125 us -> 98.1 us (0.78)
  Pallas kernels: 118 us -> 94.7 us
  other arithmetic: 4.79 us -> 0 us
  local copies, waits for them, and re-layouts: 1.23 us -> 3.24 us
    pallas_call x1, Pallas kernels: 54.1 us -> 34.8 us  [chol_call(): pl.pallas_call(chol_kernel, out_shape=jax.ShapeDtypeStruct((1, 256), f32)...]
    pallas_call x1, Pallas kernels: 64.2 us -> 59.9 us  [gram_call(): pl.pallas_call(functools.partial(gram_kernel, n_mix, n), out_shape=jax.Sh...]
    unnamed x6 -> x14, local copies, waits for them, and re-layouts: 1.23 us -> 3.24 us
    convert_element_type x2 -> x0, other arithmetic: 1.39 us -> none  [the longest x1 0.74 us: shards(): table = jnp.where(kept[None, :], signs, 0).astype(jnp.float32)]
    reduce_sum x1 -> x0, other arithmetic: 1.38 us -> none  [shards(): own_count = jnp.sum(jnp.where(member == mix_index, counts[0], 0))]
    sub x1 -> x0, other arithmetic: 1.37 us -> none  [shards(): signs = (1 - 2 * odd) * (2 * sign_bits - 1)[None, :]]
where the time goes in v2:
time: 98.1 us; the launch traced here: 97.9 us
  Pallas kernels  94.7 us (97%)
  local copies, waits for them, and re-layouts  3.24 us (3%)
    pallas_call x1, Pallas kernels, gram_call(): pl.pallas_call(functools.partial(gram_kernel, n_mix, n), out_shape=jax.Sh...  59.9 us
    pallas_call x1, Pallas kernels, chol_call(): pl.pallas_call(chol_kernel, out_shape=jax.ShapeDtypeStruct((1, 256), f32)...  34.8 us
    unnamed x14, local copies, waits for them, and re-layouts  3.24 us

profile of v2, /device:TPU:1, one launch (start us, length us, event | category | flops | bytes accessed | tf_op | source)
XLA Modules:
  0.0 97.9 jit_solution(15029221012895656495)
XLA Ops:
  0.0 0.0 copy-start.4
  0.0 0.0 copy-start
  0.0 1.2 %copy-done = f32[256,1024]{1,0:T(8,128)S(1)} copy-done((f32[256,1024]{1,0:T(8,128)S(1)}, f32[256,1024]{1,0:T(8,128)}, u32[]{:S(2)}) %copy-start) | copy-done | bytes 1048600
  1.2 0.0 copy-start.3
  1.2 0.7 copy-done.3
  1.9 0.0 copy-start.5
  1.9 0.7 copy-done.5
  2.6 0.0 copy-start.6
  2.6 0.7 copy-done.6
  3.2 0.0 copy-start.1
  3.2 0.0 copy-start.2
  3.2 59.9 %shard_map.55.g_ref = f32[2,8,8,5,8,128]{5,4,3,2,1,0:T(8,128)S(1)} custom-call(s32[1,8]{1,0:T(1,128)S(1)} %copy-done.3, s32[1,32]{1,0:T(1,128)S(1)} %copy-done.6, s32[1,256]{1,0:T(1,128)S(1)} %bitcast.4, f32[256,1024]{1,0:T(8,128)S(1)} %copy-done), custom_call_target="tpu_custom_call" | custom-call | tf_op jit(solution)/shard_map/pallas_call | solution.py:195
  63.1 0.0 copy-done.4
  63.1 0.0 copy-done.1
  63.1 0.0 copy-done.2
  63.1 34.8 %shard_map.56 = f32[1,256]{1,0:T(1,128)} custom-call(s32[1,8]{1,0:T(1,128)S(1)} %copy-done.4, f32[2,8,8,5,8,128]{5,4,3,2,1,0:T(8,128)S(1)} %shard_map.55.g_ref, f32[64,1024]{1,0:T(8,128)S(1)} %bitcast.3, f32[256,1024]{1,0:T(8,128)S(1)} %copy-done.1), custom_call_target="tpu_custom_call" | custom-call | tf_op jit(solution)/shard_map/pallas_call | solution.py:354
Async XLA Ops:
  0.0 63.1 %copy-start.4 = (s32[1,8]{1,0:T(1,128)S(1)}, s32[1,8]{1,0:T(1,128)}, u32[]{:S(2)}) copy-start(s32[1,8]{1,0:T(1,128)} %counts_ref.3) | copy-start | bytes 100
  0.0 1.2 %copy-start = (f32[256,1024]{1,0:T(8,128)S(1)}, f32[256,1024]{1,0:T(8,128)}, u32[]{:S(2)}) copy-start(f32[256,1024]{1,0:T(8,128)} %x_ref.3) | copy-start | bytes 3145732
  1.2 0.7 copy-start.3
  1.9 0.7 copy-start.5
  2.6 0.7 copy-start.6
  3.2 59.9 %copy-start.1 = (f32[256,1024]{1,0:T(8,128)S(1)}, f32[256,1024]{1,0:T(8,128)}, u32[]{:S(2)}) copy-start(f32[256,1024]{1,0:T(8,128)} %x_ref.3) | copy-start | bytes 3145732
  3.2 59.9 %copy-start.2 = (f32[1024,64]{0,1:T(8,128)S(1)}, f32[1024,64]{0,1:T(8,128)}, u32[]{:S(2)}) copy-start(f32[1024,64]{0,1:T(8,128)} %param.9) | copy-start | bytes 786436

commit v3 on v2

--- a/solution.py
+++ b/solution.py
@@ -95,8 +95,8 @@
     sent += got
     s_all[m] = functools.reduce(jnp.add, [r1[b] for b in range(n_mix)])
     got = []
-    for d in range(1, n_mix):
-        got.append(send(s_all.at[m], s_all.at[m], s2.at[d], v2.at[d], mix_peer(d)))
+    for d in range(1, n_off):
+        got.append(send(s_all.at[m], s_all.at[m], s2.at[d], v2.at[d], mix_peer(n_mix - d)))
     for copy in got:
         copy.wait_recv()
     sent += got
@@ -183,28 +183,6 @@
         copy.wait_recv()
     for copy in sent + across + list(moves.values()):
         copy.wait_send()
-
-
-def gram_call(n_mix, n, counts, samples, bits, x):
-    vm = pl.BlockSpec(memory_space=pltpu.VMEM)
-    sm = pl.BlockSpec(memory_space=pltpu.SMEM)
-    n_off, piece, k = n_mix // 2 + 1, 128 // (2 * n), samples.shape[1]
-    f32 = jnp.float32
-    dma = pltpu.SemaphoreType.DMA
-    pair = lambda *s: [dma(s), dma(s)]
-    return pl.pallas_call(
-        functools.partial(gram_kernel, n_mix, n),
-        out_shape=jax.ShapeDtypeStruct((2, n, n_mix, n_off, piece, 128), f32),
-        in_specs=[sm, sm, vm, vm], out_specs=vm,
-        scratch_shapes=[
-            pltpu.VMEM((n_mix, k, 128), f32), pltpu.VMEM((n_mix, k, 128), f32), pltpu.VMEM((n_mix, k, 128), f32),
-            pltpu.VMEM((2, n, n_off, piece, 128), f32), pltpu.VMEM((2, n, n_off, piece, 128), f32),
-            pltpu.VMEM((2, n_off, piece, 128), f32), pltpu.VMEM((2, n, n_off, piece, 128), f32),
-            pltpu.VMEM((2, n_mix, n_off, piece, 128), f32),
-            *pair(n_mix), *pair(n_mix), *pair(2, n), *pair(2, n), *pair(2, n_mix // 2),
-            *pair(2, n // 2 + 1, CHUNKS), *pair(2, n // 2 + 1, CHUNKS), dma(())],
-        compiler_params=pltpu.CompilerParams(collective_id=0, has_side_effects=True, vmem_limit_bytes=32 * 1024 * 1024),
-    )(counts, samples, bits, x)
 
 
 def mm(a, b, dims):
@@ -348,25 +326,41 @@
     o_ref[...] = jnp.where(slot < count, jnp.sum(proj * proj, axis=0, keepdims=True), 0.0)
 
 
-def chol_call(counts, g, gt, x):
+def fused_kernel(n_mix, n, counts_ref, samples_ref, bits_ref, x_ref, gt_ref, o_ref, g_ref, *scratch):
+    gram_kernel(n_mix, n, counts_ref, samples_ref, bits_ref, x_ref, g_ref, *scratch[:-10])
+    chol_kernel(counts_ref, g_ref, gt_ref, x_ref, o_ref, *scratch[-10:])
+
+
+def fused_call(n_mix, n, counts, samples, bits, x, gt):
     vm = pl.BlockSpec(memory_space=pltpu.VMEM)
+    sm = pl.BlockSpec(memory_space=pltpu.SMEM)
+    n_off, piece, k = n_mix // 2 + 1, 128 // (2 * n), samples.shape[1]
     f32, bf16 = jnp.float32, jnp.bfloat16
+    dma = pltpu.SemaphoreType.DMA
+    pair = lambda *s: [dma(s), dma(s)]
     return pl.pallas_call(
-        chol_kernel,
+        functools.partial(fused_kernel, n_mix, n),
         out_shape=jax.ShapeDtypeStruct((1, 256), f32),
-        in_specs=[pl.BlockSpec(memory_space=pltpu.SMEM)] + [vm] * 3, out_specs=vm,
-        scratch_shapes=[pltpu.VMEM((1024, 1024), f32), pltpu.VMEM((4, 256, 256), f32), pltpu.VMEM((128, 128), f32),
-                        pltpu.VMEM((128, 128), f32), pltpu.VMEM((64, 1024), f32), pltpu.VMEM((64, 1024), f32),
-                        pltpu.VMEM((128, 768), bf16), pltpu.VMEM((1024, 768), bf16), pltpu.VMEM((1024, 768), bf16),
-                        pltpu.VMEM((8, 128), f32)],
-        compiler_params=pltpu.CompilerParams(vmem_limit_bytes=48 * 1024 * 1024),
-    )(counts, g, gt, x)
+        in_specs=[sm, sm, vm, vm, vm], out_specs=vm,
+        scratch_shapes=[
+            pltpu.VMEM((2, n, n_mix, n_off, piece, 128), f32),
+            pltpu.VMEM((n_mix, k, 128), f32), pltpu.VMEM((n_mix, k, 128), f32), pltpu.VMEM((n_mix, k, 128), f32),
+            pltpu.VMEM((2, n, n_off, piece, 128), f32), pltpu.VMEM((2, n, n_off, piece, 128), f32),
+            pltpu.VMEM((2, n_off, piece, 128), f32), pltpu.VMEM((2, n, n_off, piece, 128), f32),
+            pltpu.VMEM((2, n_mix, n_off, piece, 128), f32),
+            *pair(n_mix), *pair(n_mix), *pair(2, n), *pair(2, n), *pair(2, n_mix // 2),
+            *pair(2, n // 2 + 1, CHUNKS), *pair(2, n // 2 + 1, CHUNKS), dma(()),
+            pltpu.VMEM((1024, 1024), f32), pltpu.VMEM((4, 256, 256), f32), pltpu.VMEM((128, 128), f32),
+            pltpu.VMEM((128, 128), f32), pltpu.VMEM((64, 1024), f32), pltpu.VMEM((64, 1024), f32),
+            pltpu.VMEM((128, 768), bf16), pltpu.VMEM((1024, 768), bf16), pltpu.VMEM((1024, 768), bf16),
+            pltpu.VMEM((8, 128), f32)],
+        compiler_params=pltpu.CompilerParams(collective_id=0, has_side_effects=True, vmem_limit_bytes=48 * 1024 * 1024),
+    )(counts, samples, bits, x, gt)
 
 
 def shards(matrix, counts, sign_bits, samples, gaussian):
     n_mix, n_dp = lax.axis_size("mix"), lax.axis_size("dp")
-    grams = gram_call(n_mix, math.isqrt(n_dp), counts, samples, sign_bits[None, :], matrix)
-    return chol_call(counts, grams, gaussian.T, matrix)[0]
+    return fused_call(n_mix, math.isqrt(n_dp), counts, samples, sign_bits[None, :], matrix, gaussian.T)[0]
 
 
 def solution(mesh):

time: 98.1 us -> 96.8 us (0.987)
  Pallas kernels: 94.7 us -> 93.1 us
    pallas_call x2 -> x1, Pallas kernels: 94.7 us -> 93.1 us  [fused_call(): pl.pallas_call(functools.partial(fused_kernel, n_mix, n), out_shape=jax.S...]
    unnamed x14 -> x11, local copies, waits for them, and re-layouts: 3.24 us -> 3.43 us
where the time goes in v3:
time: 96.8 us; the launch traced here: 96.6 us
  Pallas kernels  93.1 us (96%)
  local copies, waits for them, and re-layouts  3.43 us (4%)
    pallas_call x1, Pallas kernels, fused_call(): pl.pallas_call(functools.partial(fused_kernel, n_mix, n), out_shape=jax.S...  93.1 us
    unnamed x11, local copies, waits for them, and re-layouts  3.43 us

profile of v3, /device:TPU:1, one launch (start us, length us, event | category | flops | bytes accessed | tf_op | source)
XLA Modules:
  0.0 96.6 jit_solution(13335239652352583273)
XLA Ops:
  0.0 0.0 copy-start.4
  0.0 0.0 copy-start.2
  0.0 0.0 copy-start.3
  0.0 0.6 copy-done.4
  0.7 0.0 copy-done.2
  0.7 0.0 copy-done.3
  0.7 0.0 copy-start
  0.7 1.2 %copy-done = f32[256,1024]{1,0:T(8,128)S(1)} copy-done((f32[256,1024]{1,0:T(8,128)S(1)}, f32[256,1024]{1,0:T(8,128)}, u32[]{:S(2)}) %copy-start) | copy-done | bytes 1048600
  1.9 0.0 copy-start.1
  1.9 0.9 copy-done.1
  2.9 93.1 %shard_map.55 = f32[1,256]{1,0:T(1,128)S(1)} custom-call(s32[1,8]{1,0:T(1,128)S(1)} %copy-done.3, s32[1,32]{1,0:T(1,128)S(1)} %copy-done.4, s32[1,256]{1,0:T(1,128)S(1)} %bitcast.5, f32[256,1024]{1,0:T(8,128)S(1)} %copy-done, f32[64,1024]{1,0:T(8,128)S(1)} %bitcast.3), custom_call_target="tpu_custom_call" | custom-call | tf_op jit(solution)/shard_map/pallas_call | solution.py:341
  96.0 0.6 copy.7
Async XLA Ops:
  0.0 0.7 copy-start.4
  0.0 0.7 copy-start.2
  0.0 0.7 copy-start.3
  0.7 1.2 %copy-start = (f32[256,1024]{1,0:T(8,128)S(1)}, f32[256,1024]{1,0:T(8,128)}, u32[]{:S(2)}) copy-start(f32[256,1024]{1,0:T(8,128)} %x_ref.1) | copy-start | bytes 3145732
  1.9 0.9 copy-start.1

commit v4 on v3

v4 whole, which is shorter than its diff:
```python
import functools
import math

import jax
import jax.numpy as jnp
from jax import lax
from jax.experimental import pallas as pl
from jax.experimental.pallas import tpu as pltpu
from jax.sharding import PartitionSpec as P

HI = lax.Precision.HIGHEST
NN = (((1,), (0,)), ((), ()))
NT = (((1,), (1,)), ((), ()))
TN = (((0,), (0,)), ((), ()))
MESH = pl.DeviceIdType.MESH
TILES = [(i, j) for j in range(8) for i in range(j, 8)]
SLOTS = 5
WAVES = ((0, 1), (1, 4))
PASSES = ((0, 1), (1, 1), (2, 1), (3, 2))


def own_rows(counts_ref, n_mix):
    m = lax.axis_index("mix")
    first, count = jnp.int32(0), jnp.int32(0)
    for i in range(n_mix):
        first = first + jnp.where(i < m, counts_ref[0, i], 0)
        count = count + jnp.where(i == m, counts_ref[0, i], 0)
    return first, count


def mm(a, b, dims):
    return lax.dot_general(a, b, dims, precision=HI, preferred_element_type=jnp.float32)


def split(x):
    high = x.astype(jnp.bfloat16)
    rest = x - high.astype(jnp.float32)
    mid = rest.astype(jnp.bfloat16)
    return high, mid, (rest - mid.astype(jnp.float32)).astype(jnp.bfloat16)


def left_terms(x):
    high, mid, low = split(x)
    return jnp.concatenate([high, high, mid, high, low, mid], axis=1)


def right_terms(x):
    high, mid, low = split(x)
    return jnp.concatenate([high, mid, high, low, high, mid], axis=1)


def wide(a, b):
    return lax.dot_general(a, b, NT, preferred_element_type=jnp.float32)


def mm3(a, b, dims):
    ah, bh = a.astype(jnp.bfloat16), b.astype(jnp.bfloat16)
    al = (a - ah.astype(jnp.float32)).astype(jnp.bfloat16)
    bl = (b - bh.astype(jnp.float32)).astype(jnp.bfloat16)
    dot = functools.partial(lax.dot_general, dimension_numbers=dims, preferred_element_type=jnp.float32)
    return dot(ah, bh) + (dot(ah, bl) + dot(al, bh))


def factor_inverse(d_ref, t_ref, zero):
    shape = (8, 128)
    lane = lax.broadcasted_iota(jnp.int32, shape, 1)
    sub = lax.broadcasted_iota(jnp.int32, shape, 0)
    tiles = [d_ref[8 * t:8 * t + 8, :] for t in range(16)]
    lanes_of = lambda x, c: jnp.broadcast_to(x[:, c:c + 1], shape)
    rows_of = lambda x, r: jnp.broadcast_to(x[r:r + 1, :], shape)
    cols = [lanes_of(tiles[0], j) + zero for j in range(8)]
    for t in range(16):
        base = 8 * t
        inside = (lane >= base) & (lane < base + 8)
        below = [[lanes_of(tiles[u], base + j) for j in range(8)] for u in range(t + 1, 16)]
        if t < 15:
            x = [b + zero for b in below[0]]
            ahead = [lanes_of(tiles[t + 1], base + 8 + j) + zero for j in range(8)]
        row = jnp.where(inside, jnp.where(lane == base + sub, 1.0, 0.0), tiles[t])
        low, inv_col, piv_col = {}, zero, zero + 1.0
        for k in range(8):
            pivot = rows_of(cols[k], k)
            inv = 1.0 / pivot
            factor = cols[k] * inv
            for j in range(k + 1, 8):
                cols[j] = cols[j] - factor * rows_of(cols[k], j)
                low[j, k] = rows_of(factor, j)
            inv_col = jnp.where(sub == k, inv, inv_col)
            piv_col = jnp.where(sub == k, pivot, piv_col)
            if k < 7:
                row = row - jnp.where(sub > k, factor, 0.0) * rows_of(row, k)
            if t < 15:
                y = x[k] * inv
                ahead = [ahead[j] - y * rows_of(x[k], j) for j in range(8)]
                for i in range(k + 1, 8):
                    x[i] = x[i] - low[i, k] * x[k]
        t_ref[base:base + 8, :] = jnp.where(lane <= base + sub, row * lax.rsqrt(piv_col), 0.0)
        if t == 15:
            break
        cols = ahead
        row = row * inv_col
        solved = [rows_of(row, k) for k in range(8)]
        for k in range(7, 0, -1):
            for j in range(k):
                solved[j] = solved[j] - low[k, j] * solved[k]
        for u in range(t + 1, 16):
            acc = jnp.where(inside, 0.0, tiles[u])
            for k in range(8):
                acc = acc - below[u - t - 1][k] * solved[k]
            tiles[u] = acc


def is_equal(a, b):
    return 1 - jnp.minimum(1, jnp.maximum(a - b, b - a))


def fused_kernel(n_mix, n, counts_ref, samples_ref, bits_ref, x_ref, gt_ref, o_ref, g_ref,
                 part, r1, s_all, w0, w1, r30, r31, q0, q1, r40, r41, f0, f1, *rest):
    (s1, v1, s2, v2, s3, v3, s4, v4, s5, v5, s6, v6, s7, v7, local,
     a_ref, tp_ref, t_ref, d_ref, acc_ref, xt_ref, tr_ref, vl_ref, vr_ref, z_ref) = rest
    w, r3, q, r4, f = (w0, w1), (r30, r31), (q0, q1), (r40, r41), (f0, f1)
    dp, m = lax.axis_index("dp"), lax.axis_index("mix")
    y, z = dp // n, dp % n
    x, core = m // 2, m % 2
    nx = n_mix // 2
    nb = n_mix
    size = 128 * nb
    piece = 128 // (2 * n)
    capacity, picks = x_ref.shape[0], samples_ref.shape[1]

    def mix_peer(d):
        return (dp, (m + d) % n_mix)

    def y_peer(d):
        return (((y + d) % n) * n + z, m)

    def z_peer(d):
        return (y * n + (z + d) % n, m)

    barrier = pltpu.get_barrier_semaphore()
    for d in range(1, n_mix):
        pl.semaphore_signal(barrier, inc=1, device_id=mix_peer(d), device_id_type=MESH)
    for d in range(1, n):
        pl.semaphore_signal(barrier, inc=1, device_id=y_peer(d), device_id_type=MESH)
        pl.semaphore_signal(barrier, inc=1, device_id=z_peer(d), device_id_type=MESH)

    def remote(src, dst, ssem, rsem, peer):
        return pltpu.make_async_remote_copy(src_ref=src, dst_ref=dst, send_sem=ssem, recv_sem=rsem,
                                            device_id=peer, device_id_type=MESH)

    sent = []

    def send(*what):
        copy = remote(*what)
        copy.start()
        sent.append(copy)
        return copy

    def received(copies):
        for copy in copies:
            copy.wait_recv()

    first, count = own_rows(counts_ref, n_mix)
    slot = lax.broadcasted_iota(jnp.int32, (8, capacity), 1)
    row = lax.broadcasted_iota(jnp.int32, (8, capacity), 0)
    sign = jnp.where(slot < count, 2 * bits_ref[...] - 1, 0)
    table = []
    for base in range(0, picks, 8):
        sample = jnp.zeros((8, capacity), jnp.int32)
        for i in range(8):
            sample = jnp.where(row == i, samples_ref[0, base + i], sample)
        odd = jnp.bitwise_and(sample, first + slot)
        for shift in (8, 4, 2, 1):
            odd = jnp.bitwise_xor(odd, jnp.right_shift(odd, shift))
        table.append(jnp.where(jnp.bitwise_and(odd, 1) == 1, -sign, sign))
    table = jnp.concatenate(table, axis=0).astype(jnp.float32).astype(jnp.bfloat16)
    scale = 1.0 / math.sqrt(n_mix * 128 * picks)
    for b in range(n_mix):
        rest_of = x_ref[:, 128 * b:128 * b + 128]
        total = None
        for _ in range(3):
            term = rest_of.astype(jnp.bfloat16)
            rest_of = rest_of - term.astype(jnp.float32)
            product = lax.dot_general(table, term, NN, preferred_element_type=jnp.float32)
            total = product if total is None else total + product
        part[b] = total * scale
    pl.semaphore_wait(barrier, n_mix - 1 + 2 * (n - 1))

    got = []
    for d in range(1, n_mix):
        p = (m + d) % n_mix
        got.append(send(part.at[p], r1.at[m], s1.at[d], v1.at[d], mix_peer(d)))
    r1[m] = part[m]
    a_ref[...] = jnp.zeros_like(a_ref)
    tp_ref[...] = jnp.zeros_like(tp_ref)
    tr_ref[...] = jnp.zeros_like(tr_ref)
    z_ref[...] = jnp.zeros_like(z_ref)
    received(got)
    s_all[m] = functools.reduce(jnp.add, [r1[b] for b in range(n_mix)])
    received([send(s_all.at[m], s_all.at[m], s2.at[d], v2.at[d], mix_peer(d)) for d in range(1, n_mix)])

    def tiles(k):
        start, many = WAVES[k]
        for s in range(start, start + many):
            own = [TILES[min(n_mix * s + b, len(TILES) - 1)] for b in range(n_mix)]
            i = sum(own[b][0] * is_equal(m, b) for b in range(n_mix))
            j = sum(own[b][1] * is_equal(m, b) for b in range(n_mix))
            tile = lax.dot_general(s_all[i], s_all[j], TN, precision=HI, preferred_element_type=jnp.float32)
            for h in range(2):
                for p in range(n):
                    r = (h * n + p) * piece
                    w[k][h, p, s - start] = tile[r:r + piece]

    def reduce_first(k):
        got = []
        for d in range(1, n):
            got.append(send(w[k].at[0, (y + d) % n], r3[k].at[0, y], s3.at[k, 0, d], v3.at[k, 0, d], y_peer(d)))
            got.append(send(w[k].at[1, (z + d) % n], r3[k].at[1, z], s3.at[k, 1, d], v3.at[k, 1, d], z_peer(d)))
        r3[k][0, y] = w[k][0, y]
        r3[k][1, z] = w[k][1, z]
        return got

    def reduce_second(k, got):
        received(got)
        for h in range(2):
            q[k][h] = functools.reduce(jnp.add, [r3[k][h, p] for p in range(n)])
        got = []
        for d in range(1, n):
            got.append(send(q[k].at[0], r4[k].at[0, z], s4.at[k, 0, d], v4.at[k, 0, d], z_peer(d)))
            got.append(send(q[k].at[1], r4[k].at[1, y], s4.at[k, 1, d], v4.at[k, 1, d], y_peer(d)))
        r4[k][0, z] = q[k][0]
        r4[k][1, y] = q[k][1]
        return got

    def gather_mix(k, got):
        received(got)
        for h in range(2):
            f[k][h, m] = functools.reduce(jnp.add, [r4[k][h, p] for p in range(n)])
        got = []
        for d in range(nx):
            column = ((x + d) % nx) * 2
            if d:
                got.append(send(f[k].at[core, m], f[k].at[core, m], s5.at[k, 0, d], v5.at[k, 0, d], (dp, column + core)))
            got.append(send(f[k].at[1 - core, m], f[k].at[1 - core, m], s5.at[k, 1, d], v5.at[k, 1, d], (dp, column + 1 - core)))
        return got

    place = y + core * (z - y)
    sibling = (dp, m + 1 - 2 * core)

    def source(k):
        start, many = PASSES[k]
        return f0.at[core] if k == 0 else f1.at[core, :, pl.ds(start - 1, many)]

    def block(k, d):
        start, many = PASSES[k]
        return g_ref.at[core, (place + n - d) % n, :, pl.ds(start, many)]

    def place_copy(k, d):
        peer = (((y + d * (1 - core)) % n) * n + (z + d * core) % n, m)
        return remote(source(k), block(k, 0), s6.at[k, d], v6.at[k, d], peer)

    def own_copy(k):
        return pltpu.make_async_copy(source(k), block(k, 0), local.at[k])

    def core_copy(k, d):
        return remote(block(k, d) if d else source(k), block(k, d), s7.at[k, d], v7.at[k, d], sibling)

    def gather_places(k):
        for d in range(1, n):
            place_copy(k, d).start()
        core_copy(k, 0).start()
        own_copy(k).start()

    def pass_on(k):
        for d in range(1, n):
            place_copy(k, d).wait_recv()
            core_copy(k, d).start()

    def absorb(k):
        own_copy(k).wait()
        for d in range(n):
            core_copy(k, d).wait_recv()
        start, many = PASSES[k]
        for s in range(start, start + many):
            for b in range(n_mix):
                if n_mix * s + b < len(TILES):
                    i, j = TILES[n_mix * s + b]
                    for h in range(2):
                        for p in range(n):
                            r = i * 128 + (h * n + p) * piece
                            a_ref[r:r + piece, 128 * j:128 * j + 128] = a_ref[r:r + piece, 128 * j:128 * j + 128] + g_ref[h, p, b, s]

    tiles(0)
    early = reduce_first(0)
    tiles(1)
    late = reduce_first(1)
    early = reduce_second(0, early)
    late = reduce_second(1, late)
    early = gather_mix(0, early)
    received(early)
    gather_places(0)
    late = gather_mix(1, late)
    received(late)
    for k in range(1, len(PASSES)):
        gather_places(k)
    pass_on(0)
    absorb(0)
    d_ref[...] = a_ref[:128, :128]

    def step(kb, carry):
        past = pl.multiple_of(jnp.maximum(kb - 1, 0) * 128, 128)
        here = pl.multiple_of(kb * 128, 128)
        col = a_ref[:, pl.ds(past, 128)]
        row_ids = lax.broadcasted_iota(jnp.int32, (size, 128), 0)
        mine = (row_ids >= here) & (kb > 0)
        v = jnp.where(mine, wide(left_terms(col), tr_ref[...]), 0.0)
        a_ref[:, pl.ds(past, 128)] = jnp.where(mine, v, col)
        vl_ref[...] = left_terms(v)
        vr_ref[...] = right_terms(v)
        for left in range(0, size, 256):
            update = wide(vl_ref[left:, :], vr_ref[left:left + 256, :])
            a_ref[left:, left:left + 256] = a_ref[left:, left:left + 256] - update
        factor_inverse(d_ref, t_ref, z_ref[...])
        tri = t_ref[...]
        half = pl.multiple_of((kb % 2) * 128, 128)
        tp_ref[kb // 2, pl.ds(half, 128), pl.ds(half, 128)] = tri
        tr_ref[...] = right_terms(tri)

        return carry

    def next_block(kb, carry):
        here = pl.multiple_of(kb * 128, 128)
        then = pl.multiple_of(jnp.minimum(kb + 1, nb - 1) * 128, 128)
        v = wide(left_terms(a_ref[pl.ds(then, 128), pl.ds(here, 128)]), tr_ref[...])
        d_ref[...] = a_ref[pl.ds(then, 128), pl.ds(then, 128)] - wide(left_terms(v), right_terms(v))
        return carry

    for kb in range(3):
        lax.fori_loop(kb, kb + 1, step, 0)
        pass_on(kb + 1)
        if kb == 0:
            absorb(1)
        if kb == 2:
            absorb(2)
        next_block(kb, 0)
    lax.fori_loop(3, 4, step, 0)
    absorb(3)
    next_block(3, 0)
    lax.fori_loop(4, nb, lambda kb, carry: next_block(kb, step(kb, carry)), 0)
    for p in range(nb // 2):
        s = 256 * p
        link = mm3(a_ref[s + 128:s + 256, s:s + 128], tp_ref[p, :128, :128], NN)
        tp_ref[p, 128:, :128] = -mm3(tp_ref[p, 128:, 128:], link, NN)
    acc_ref[...] = gt_ref[...]
    for p in range(nb // 2 - 1, -1, -1):
        s = slice(256 * p, 256 * p + 256)
        solved = mm3(acc_ref[:, s], tp_ref[p], NN)
        xt_ref[:, s] = solved
        if p:
            acc_ref[:, :256 * p] = acc_ref[:, :256 * p] - mm3(solved, a_ref[s, :256 * p], NN)
    proj = mm3(xt_ref[...], x_ref[...], NT)
    slot = lax.broadcasted_iota(jnp.int32, o_ref.shape, 1)
    o_ref[...] = jnp.where(slot < count, jnp.sum(proj * proj, axis=0, keepdims=True), 0.0)
    for copy in sent:
        copy.wait_send()
    for k in range(len(PASSES)):
        for d in range(n):
            if d:
                place_copy(k, d).wait_send()
            core_copy(k, d).wait_send()


def fused_call(n_mix, n, counts, samples, bits, x, gt):
    vm = pl.BlockSpec(memory_space=pltpu.VMEM)
    sm = pl.BlockSpec(memory_space=pltpu.SMEM)
    piece, k = 128 // (2 * n), samples.shape[1]
    f32, bf16 = jnp.float32, jnp.bfloat16
    dma = pltpu.SemaphoreType.DMA
    pair = lambda *s: [dma(s), dma(s)]
    waves = lambda *s: [pltpu.VMEM((*s, many, piece, 128), f32) for _, many in WAVES]
    return pl.pallas_call(
        functools.partial(fused_kernel, n_mix, n),
        out_shape=jax.ShapeDtypeStruct((1, x.shape[0]), f32),
        in_specs=[sm, sm, vm, vm, vm], out_specs=vm,
        scratch_shapes=[
            pltpu.VMEM((2, n, n_mix, SLOTS, piece, 128), f32),
            pltpu.VMEM((n_mix, k, 128), f32), pltpu.VMEM((n_mix, k, 128), f32), pltpu.VMEM((n_mix, k, 128), f32),
            *waves(2, n), *waves(2, n), *waves(2), *waves(2, n), *waves(2, n_mix),
            *pair(n_mix), *pair(n_mix), *pair(2, 2, n), *pair(2, 2, n), *pair(2, 2, n_mix // 2),
            *pair(len(PASSES), n), *pair(len(PASSES), n), dma((len(PASSES),)),
            pltpu.VMEM((1024, 1024), f32), pltpu.VMEM((4, 256, 256), f32), pltpu.VMEM((128, 128), f32),
            pltpu.VMEM((128, 128), f32), pltpu.VMEM((64, 1024), f32), pltpu.VMEM((64, 1024), f32),
            pltpu.VMEM((128, 768), bf16), pltpu.VMEM((1024, 768), bf16), pltpu.VMEM((1024, 768), bf16),
            pltpu.VMEM((8, 128), f32)],
        compiler_params=pltpu.CompilerParams(collective_id=0, has_side_effects=True, vmem_limit_bytes=48 * 1024 * 1024),
    )(counts, samples, bits, x, gt)


def shards(matrix, counts, sign_bits, samples, gaussian):
    n_mix, n_dp = lax.axis_size("mix"), lax.axis_size("dp")
    return fused_call(n_mix, math.isqrt(n_dp), counts, samples, sign_bits[None, :], matrix, gaussian.T)[0]


def solution(mesh):
    in_specs = (P(("dp", "mix"), None), P("dp", None), P(("dp", "mix")), P("dp", None), P())
    out_specs = P(("dp", "mix"))
    return jax.shard_map(shards, mesh=mesh, in_specs=in_specs, out_specs=out_specs, check_vma=False)
```

time: 96.8 us -> 86 us (0.89)
  Pallas kernels: 93.1 us -> 82.3 us
    pallas_call x1, Pallas kernels: 93.1 us -> 82.3 us  [fused_call(): pl.pallas_call(functools.partial(fused_kernel, n_mix, n), out_shape=jax.S...]
where the time goes in v4:
time: 86 us; the launch traced here: 85.8 us
  Pallas kernels  82.3 us (96%)
  local copies, waits for them, and re-layouts  3.43 us (4%)
    pallas_call x1, Pallas kernels, fused_call(): pl.pallas_call(functools.partial(fused_kernel, n_mix, n), out_shape=jax.S...  82.3 us
    unnamed x11, local copies, waits for them, and re-layouts  3.43 us

profile of v4, /device:TPU:1, one launch (start us, length us, event | category | flops | bytes accessed | tf_op | source)
XLA Modules:
  0.0 85.8 jit_solution(1752526809238970553)
XLA Ops:
  0.0 0.0 copy-start.4
  0.0 0.0 copy-start.2
  0.0 0.0 copy-start.3
  0.0 0.6 copy-done.4
  0.7 0.0 copy-done.2
  0.7 0.0 copy-done.3
  0.7 0.0 copy-start
  0.7 1.2 %copy-done = f32[256,1024]{1,0:T(8,128)S(1)} copy-done((f32[256,1024]{1,0:T(8,128)S(1)}, f32[256,1024]{1,0:T(8,128)}, u32[]{:S(2)}) %copy-start) | copy-done | bytes 1048600
  1.9 0.0 copy-start.1
  1.9 0.9 %copy-done.1 = f32[1024,64]{0,1:T(8,128)S(1)} copy-done((f32[1024,64]{0,1:T(8,128)S(1)}, f32[1024,64]{0,1:T(8,128)}, u32[]{:S(2)}) %copy-start.1) | copy-done | bytes 262168
  2.9 82.3 %shard_map.55 = f32[1,256]{1,0:T(1,128)S(1)} custom-call(s32[1,8]{1,0:T(1,128)S(1)} %copy-done.3, s32[1,32]{1,0:T(1,128)S(1)} %copy-done.4, s32[1,256]{1,0:T(1,128)S(1)} %bitcast.5, f32[256,1024]{1,0:T(8,128)S(1)} %copy-done, f32[64,1024]{1,0:T(8,128)S(1)} %bitcast.3), custom_call_target="tpu_custom_call" | custom-call | tf_op jit(solution)/shard_map/pallas_call | solution.py:381
  85.2 0.6 copy.7
Async XLA Ops:
  0.0 0.7 copy-start.4
  0.0 0.7 copy-start.2
  0.0 0.7 copy-start.3
  0.7 1.2 %copy-start = (f32[256,1024]{1,0:T(8,128)S(1)}, f32[256,1024]{1,0:T(8,128)}, u32[]{:S(2)}) copy-start(f32[256,1024]{1,0:T(8,128)} %x_ref.1) | copy-start | bytes 3145732
  1.9 0.9 %copy-start.1 = (f32[1024,64]{0,1:T(8,128)S(1)}, f32[1024,64]{0,1:T(8,128)}, u32[]{:S(2)}) copy-start(f32[1024,64]{0,1:T(8,128)} %param.9) | copy-start | bytes 786436

commit v5 on v4

--- a/solution.py
+++ b/solution.py
@@ -193,7 +193,6 @@
     r1[m] = part[m]
     a_ref[...] = jnp.zeros_like(a_ref)
     tp_ref[...] = jnp.zeros_like(tp_ref)
-    tr_ref[...] = jnp.zeros_like(tr_ref)
     z_ref[...] = jnp.zeros_like(z_ref)
     received(got)
     s_all[m] = functools.reduce(jnp.add, [r1[b] for b in range(n_mix)])
@@ -308,11 +307,11 @@
     d_ref[...] = a_ref[:128, :128]
 
     def step(kb, carry):
-        past = pl.multiple_of(jnp.maximum(kb - 1, 0) * 128, 128)
+        past = pl.multiple_of((kb - 1) * 128, 128)
         here = pl.multiple_of(kb * 128, 128)
         col = a_ref[:, pl.ds(past, 128)]
         row_ids = lax.broadcasted_iota(jnp.int32, (size, 128), 0)
-        mine = (row_ids >= here) & (kb > 0)
+        mine = row_ids >= here
         v = jnp.where(mine, wide(left_terms(col), tr_ref[...]), 0.0)
         a_ref[:, pl.ds(past, 128)] = jnp.where(mine, v, col)
         vl_ref[...] = left_terms(v)
@@ -320,6 +319,9 @@
         for left in range(0, size, 256):
             update = wide(vl_ref[left:, :], vr_ref[left:left + 256, :])
             a_ref[left:, left:left + 256] = a_ref[left:, left:left + 256] - update
+        return factor(kb, carry)
+
+    def factor(kb, carry):
         factor_inverse(d_ref, t_ref, z_ref[...])
         tri = t_ref[...]
         half = pl.multiple_of((kb % 2) * 128, 128)
@@ -336,7 +338,7 @@
         return carry
 
     for kb in range(3):
-        lax.fori_loop(kb, kb + 1, step, 0)
+        lax.fori_loop(kb, kb + 1, step if kb else factor, 0)
         pass_on(kb + 1)
         if kb == 0:
             absorb(1)

time: 86 us -> 85.9 us (level)
  no operation moved by 1% of the time
where the time goes in v5:
time: 85.9 us; the launch traced here: 85.8 us
  Pallas kernels  82.3 us (96%)
  local copies, waits for them, and re-layouts  3.43 us (4%)
    pallas_call x1, Pallas kernels, fused_call(): pl.pallas_call(functools.partial(fused_kernel, n_mix, n), out_shape=jax.S...  82.3 us
    unnamed x11, local copies, waits for them, and re-layouts  3.43 us

profile of v5, /device:TPU:1, one launch (start us, length us, event | category | flops | bytes accessed | tf_op | source)
XLA Modules:
  0.0 85.8 jit_solution(17076000525998912504)
XLA Ops:
  0.0 0.0 copy-start.4
  0.0 0.0 copy-start.2
  0.0 0.0 copy-start.3
  0.0 0.6 copy-done.4
  0.7 0.0 copy-done.2
  0.7 0.0 copy-done.3
  0.7 0.0 copy-start
  0.7 1.2 %copy-done = f32[256,1024]{1,0:T(8,128)S(1)} copy-done((f32[256,1024]{1,0:T(8,128)S(1)}, f32[256,1024]{1,0:T(8,128)}, u32[]{:S(2)}) %copy-start) | copy-done | bytes 1048600
  1.9 0.0 copy-start.1
  1.9 0.9 %copy-done.1 = f32[1024,64]{0,1:T(8,128)S(1)} copy-done((f32[1024,64]{0,1:T(8,128)S(1)}, f32[1024,64]{0,1:T(8,128)}, u32[]{:S(2)}) %copy-start.1) | copy-done | bytes 262168
  2.9 82.3 %shard_map.55 = f32[1,256]{1,0:T(1,128)S(1)} custom-call(s32[1,8]{1,0:T(1,128)S(1)} %copy-done.3, s32[1,32]{1,0:T(1,128)S(1)} %copy-done.4, s32[1,256]{1,0:T(1,128)S(1)} %bitcast.5, f32[256,1024]{1,0:T(8,128)S(1)} %copy-done, f32[64,1024]{1,0:T(8,128)S(1)} %bitcast.3), custom_call_target="tpu_custom_call" | custom-call | tf_op jit(solution)/shard_map/pallas_call | solution.py:383
  85.2 0.6 copy.7
Async XLA Ops:
  0.0 0.7 copy-start.4
  0.0 0.7 copy-start.2
  0.0 0.7 copy-start.3
  0.7 1.2 %copy-start = (f32[256,1024]{1,0:T(8,128)S(1)}, f32[256,1024]{1,0:T(8,128)}, u32[]{:S(2)}) copy-start(f32[256,1024]{1,0:T(8,128)} %x_ref.1) | copy-start | bytes 3145732
  1.9 0.9 %copy-start.1 = (f32[1024,64]{0,1:T(8,128)S(1)}, f32[1024,64]{0,1:T(8,128)}, u32[]{:S(2)}) copy-start(f32[1024,64]{0,1:T(8,128)} %param.9) | copy-start | bytes 786436
